TPU v7x, 32 devices: a whole 2x2x4 slice. The times are simulated.
32 devices in a mesh: bin: 8 (over z, y), sky: 4 (over x, core).
Axes of the slice: x: 2, y: 2, z: 4, core: 2. Of those that a mesh axis runs over, the one named last changes fastest.
Arguments:
- lensing_maps: bfloat16 [8, 32, 8192], P('bin', 'sky')
- filter_taps: float32 [5, 17], replicated, may hold values from -1.5 to 1.5
- survey_mask: int32 [4, 64], P('sky'), may hold values 0 or 1
- bin_pairs: int32 [36, 2], replicated, may hold values from 0 to 7, as said below
- target_corr: float32 [36, 5, 4], replicated, may hold values from -3 to 3
- pair_weight: float32 [36, 5, 4], replicated, may hold values from 0.3 to 3
Outputs:
- corr_table: float32 [36, 5, 4], replicated
- map_gradient: float32 [8, 32, 8192], P('bin', 'sky')
Inputs may be any that keep to these rules, and one draw needn't show every extreme that they name: `bin_pairs`: every unordered pair of the 8 bins, a bin with itself included, is listed exactly once; the order of the list and of the two bins in a row vary.
All inputs are finite; a program needn't handle non-finite values. No bound on the sum of `survey_mask` on one device may be relied on, other than what follows from the above.
Results may differ from a plain program's by a relative error of at most 0.0015.
Values may be sent and summed in bfloat16 or wider, within the bound.
A program may use at most 64 MiB of HBM per device.

v0:
```python
import jax
import jax.numpy as jnp
from jax import lax
from jax.sharding import PartitionSpec as P

HIGH = lax.Precision.HIGHEST


def with_halo(block, sides, width):
    for axis, dim in sides:
        count = lax.axis_size(axis)
        forward = [(i, i + 1) for i in range(count - 1)]
        backward = [(target, source) for source, target in forward]
        low = lax.ppermute(
            lax.slice_in_dim(block, block.shape[dim] - width, None, axis=dim), axis, forward
        )
        high = lax.ppermute(lax.slice_in_dim(block, 0, width, axis=dim), axis, backward)
        block = jnp.concatenate([low, block, high], axis=dim)
    return block


def shifted(value, axis, steps):
    count = lax.axis_size(axis)
    pairs = [(source, (source + steps) % count) for source in range(count)]
    return lax.ppermute(value, axis, pairs)


def expand_mask(survey_mask):
    values = survey_mask.astype(jnp.float32)
    tiles_x, tiles_y = values.shape
    return jnp.broadcast_to(values[:, None, :, None], (tiles_x, 8, tiles_y, 128)).reshape(
        tiles_x * 8, tiles_y * 128
    )


def smooth(haloed, filter_taps, row_count):
    tap_count = filter_taps.shape[1]
    half_width = (tap_count - 1) // 2
    widened = haloed.astype(jnp.float32)
    across = filter_taps[:, 0, None, None] * widened[None, 0:row_count]
    for a in range(1, tap_count):
        across = across + filter_taps[:, a, None, None] * widened[None, a : a + row_count]
    padded = jnp.pad(across, ((0, 0), (0, 0), (half_width, half_width)))
    col_count = widened.shape[1]
    result = filter_taps[:, 0, None, None] * padded[:, :, 0:col_count]
    for c in range(1, tap_count):
        result = result + filter_taps[:, c, None, None] * padded[:, :, c : c + col_count]
    return result.astype(jnp.bfloat16)


def lagged(left_maps, right_maps, pixmask, lag_count):
    col_count = left_maps.shape[2]
    columns = []
    for offset in range(lag_count):
        joint_mask = pixmask[:, : col_count - offset] * pixmask[:, offset:]
        product = (
            left_maps[:, :, : col_count - offset].astype(jnp.float32)
            * right_maps[:, :, offset:].astype(jnp.float32)
            * joint_mask[None]
        )
        columns.append(jnp.sum(product, axis=(1, 2)))
    return jnp.stack(columns, axis=1)


def adjoint_lags(partner, ahead_w, behind_w, pixmask):
    col_count = partner.shape[2]
    widened = partner.astype(jnp.float32)
    totals = jnp.zeros(partner.shape, jnp.float32)
    for offset in range(ahead_w.shape[1]):
        joint_mask = pixmask[:, : col_count - offset] * pixmask[:, offset:]
        front = jnp.pad(joint_mask[None] * widened[:, :, offset:], ((0, 0), (0, 0), (0, offset)))
        back = jnp.pad(
            joint_mask[None] * widened[:, :, : col_count - offset], ((0, 0), (0, 0), (offset, 0))
        )
        totals = (
            totals + ahead_w[:, offset, None, None] * front + behind_w[:, offset, None, None] * back
        )
    return totals


def adjoint_cols(grads, filter_taps):
    tap_count = filter_taps.shape[1]
    half_width = (tap_count - 1) // 2
    col_count = grads.shape[2]
    padded = jnp.pad(grads, ((0, 0), (0, 0), (half_width, half_width)))
    result = filter_taps[:, tap_count - 1, None, None] * padded[:, :, 0:col_count]
    for c in range(1, tap_count):
        result = (
            result + filter_taps[:, tap_count - 1 - c, None, None] * padded[:, :, c : c + col_count]
        )
    return result


def adjoint_rows(widened, filter_taps, row_count):
    tap_count = filter_taps.shape[1]
    result = filter_taps[:, tap_count - 1, None, None] * widened[:, 0:row_count]
    for a in range(1, tap_count):
        result = (
            result + filter_taps[:, tap_count - 1 - a, None, None] * widened[:, a : a + row_count]
        )
    return jnp.sum(result, axis=0)


def put_block(row_hot, col_hot, values):
    return row_hot[:, None, None, None] * col_hot[None, :, None, None] * values[None, None]


def take_block(table, row_hot, col_hot):
    return jnp.einsum("i,j,ijsl->sl", row_hot, col_hot, table, precision=HIGH)


def per_device(lensing_maps, filter_taps, survey_mask, bin_pairs, target_corr, pair_weight):
    tap_count = filter_taps.shape[1]
    half_width = (tap_count - 1) // 2
    my_strip = lensing_maps[0]
    row_count, col_count = my_strip.shape
    bin_count = lax.axis_size("bin")
    sky_count = lax.axis_size("sky")
    my_bin = lax.axis_index("bin")
    lag_count = pair_weight.shape[2]
    inverse_area = 1.0 / (row_count * sky_count * col_count)
    pixmask = expand_mask(survey_mask)
    haloed = with_halo(my_strip, (("sky", 0),), half_width)
    own_maps = smooth(haloed, filter_taps, row_count)

    def forward_move(carried):
        moved = shifted(carried, "bin", 1)
        return moved

    indices = jnp.arange(bin_count, dtype=jnp.int32)
    mine_hot = (indices == my_bin).astype(jnp.float32)

    def bin_hot(k):
        return (indices == (my_bin - k) % bin_count).astype(jnp.float32)

    visit_count = bin_count - 1
    stored_init = jnp.zeros((visit_count,) + own_maps.shape, own_maps.dtype)

    def keep_visitor(stored, carried, k):
        stored = lax.dynamic_update_index_in_dim(stored, carried, k - 1, 0)
        return stored

    initial = put_block(
        mine_hot, mine_hot, lagged(own_maps, own_maps, pixmask, lag_count) * inverse_area
    )

    def advance(k, state_all):
        carried, tables, stored = state_all
        carried = forward_move(carried)
        stored = keep_visitor(stored, carried, k)
        tables = tables + put_block(
            mine_hot, bin_hot(k), lagged(own_maps, carried, pixmask, lag_count) * inverse_area
        )
        return (carried, tables, stored)

    _, tables, stored = lax.fori_loop(1, bin_count, advance, (own_maps, initial, stored_init))
    pair_table = lax.psum(tables, ("bin", "sky"))
    left_hot = (bin_pairs[:, 0:1] == indices[None, :]).astype(jnp.float32)
    right_hot = (bin_pairs[:, 1:2] == indices[None, :]).astype(jnp.float32)
    corr_table = jnp.einsum("pi,pj,ijsl->psl", left_hot, right_hot, pair_table, precision=HIGH)
    pair_grad = pair_weight * (corr_table - target_corr)
    table_grad = jnp.einsum("pi,pj,psl->ijsl", left_hot, right_hot, pair_grad, precision=HIGH)
    own_block = take_block(table_grad, mine_hot, mine_hot)
    start_grad = adjoint_lags(own_maps, own_block, own_block, pixmask)

    def partner_term(visitor, k):
        other_hot = bin_hot(k)
        return adjoint_lags(
            visitor,
            take_block(table_grad, mine_hot, other_hot),
            take_block(table_grad, other_hot, mine_hot),
            pixmask,
        )

    def reread(k, totals):
        visitor = lax.dynamic_index_in_dim(stored, k - 1, 0, keepdims=False)
        return totals + partner_term(visitor, k)

    totals = lax.fori_loop(1, visit_count + 1, reread, start_grad)
    col_pass = adjoint_cols(totals, filter_taps)
    widened = with_halo(col_pass, (("sky", 1),), half_width)
    map_grad = adjoint_rows(widened, filter_taps, row_count)
    return (corr_table, map_grad[None])


def solution(mesh):
    placed = (P("bin", "sky", None), P(), P("sky", None), P(), P(), P())
    return jax.shard_map(
        per_device,
        mesh=mesh,
        in_specs=placed,
        out_specs=(P(), P("bin", "sky", None)),
        check_vma=False,
    )
```

profile of v0, /device:TPU:9, one launch (start us, length us, event | category | flops | bytes accessed | tf_op | source)
XLA Modules:
  0.0 306.5 jit_solution(4904538330784414321)
XLA Ops:
  0.6 3.7 %collective-permute-start.1 = (bf16[8,8192]{1,0:T(8,128)(2,1)}, bf16[8,8192]{1,0:T(8,128)(2,1)S(1)}, u32[]{:S(2)}, u32[]{:S(2)}) collective-permute-start(bf16[8,8192]{1,0:T(8,128)(2,1)} %bitcast.118), channel_id=1, source_target_pairs={{0,1},{1,2},{2,3},{4,5},{5,6},{6,7},{8,9},{9,10},{10,11},{12,13},{... | collective-permute-start | bytes 393224 | tf_op jit(solution)/shard_map/ppermute | solution.py:14
  4.3 1.9 collective-permute-start.2
  8.1 1.8 slice_reduce_fusion.16
  12.1 1.8 multiply_add_fusion.4
  14.0 5.9 %fusion.112 = (f32[5,8,8192]{2,1,0:T(8,128)S(1)}, bf16[5,8,8192]{2,1,0:T(8,128)(2,1)S(1)}) fusion(f32[5]{0:T(128)S(1)} %get-tuple-element.778, f32[5]{0:T(128)S(1)} %get-tuple-element.779, f32[5]{0:T(128)S(1)} %get-tuple-element.764, f32[5]{0:T(128)S(1)} %get-tuple-element.765, f32[5]{0:T(128)S(1)} %get-tuple-element.766, f32[5]{0:T(128)S(1)} %get-tuple-element.767, ...), kind=kLoop, calls=%fused_computation.223 | loop fusion | flops 11468800 | bytes 3277140 | tf_op jit(solution)/shard_map/convert_element_type | solution.py:57
  20.8 1.7 slice_multiply_fusion.11
  22.5 2.1 slice_multiply_fusion.9
  24.6 2.1 slice_multiply_fusion.7
  27.2 143.4 %while.42 = (s32[]{:T(128)}, bf16[5,8,8192]{2,1,0:T(8,128)(2,1)}, f32[8,8,5,4]{1,3,2,0:T(4,128)S(1)}, bf16[7,5,8,8192]{3,2,1,0:T(8,128)(2,1)}, s32[]{:T(128)}, /...) while((s32[]{:T(128)}, bf16[5,8,8192]{2,1,0:T(8,128)(2,1)}, ...), condition=%wide.region_9.10_spmd.clone.clone, body=%wide.region_4.9_spmd.clone.clone.sunk | while | flops 6555130 | bytes 10627522 | solution.py:156
  28.6 14.0 %collective-permute-done = bf16[5,8,8192]{2,1,0:T(8,128)(2,1)S(1)} collective-permute-done((bf16[5,8,8192]{2,1,0:T(8,128)(2,1)}, bf16[5,8,8192]{2,1,0:T(8,128)(2,1)S(1)}, u32[]{:S(2)}, u32[]{:S(2)}) %collective-permute-start) | collective-permute-done | bytes 655392 | tf_op jit(solution)/shard_map/while/body/eval_jaxpr/ppermute | solution.py:25
  46.6 16.1 %collective-permute-done = bf16[5,8,8192]{2,1,0:T(8,128)(2,1)S(1)} collective-permute-done((bf16[5,8,8192]{2,1,0:T(8,128)(2,1)}, bf16[5,8,8192]{2,1,0:T(8,128)(2,1)S(1)}, u32[]{:S(2)}, u32[]{:S(2)}) %collective-permute-start) | collective-permute-done | bytes 655392 | tf_op jit(solution)/shard_map/while/body/eval_jaxpr/ppermute | solution.py:25
  66.4 17.7 %collective-permute-done = bf16[5,8,8192]{2,1,0:T(8,128)(2,1)S(1)} collective-permute-done((bf16[5,8,8192]{2,1,0:T(8,128)(2,1)}, bf16[5,8,8192]{2,1,0:T(8,128)(2,1)S(1)}, u32[]{:S(2)}, u32[]{:S(2)}) %collective-permute-start) | collective-permute-done | bytes 655392 | tf_op jit(solution)/shard_map/while/body/eval_jaxpr/ppermute | solution.py:25
  87.8 16.9 %collective-permute-done = bf16[5,8,8192]{2,1,0:T(8,128)(2,1)S(1)} collective-permute-done((bf16[5,8,8192]{2,1,0:T(8,128)(2,1)}, bf16[5,8,8192]{2,1,0:T(8,128)(2,1)S(1)}, u32[]{:S(2)}, u32[]{:S(2)}) %collective-permute-start) | collective-permute-done | bytes 655392 | tf_op jit(solution)/shard_map/while/body/eval_jaxpr/ppermute | solution.py:25
  108.4 18.1 %collective-permute-done = bf16[5,8,8192]{2,1,0:T(8,128)(2,1)S(1)} collective-permute-done((bf16[5,8,8192]{2,1,0:T(8,128)(2,1)}, bf16[5,8,8192]{2,1,0:T(8,128)(2,1)S(1)}, u32[]{:S(2)}, u32[]{:S(2)}) %collective-permute-start) | collective-permute-done | bytes 655392 | tf_op jit(solution)/shard_map/while/body/eval_jaxpr/ppermute | solution.py:25
  130.2 17.0 %collective-permute-done = bf16[5,8,8192]{2,1,0:T(8,128)(2,1)S(1)} collective-permute-done((bf16[5,8,8192]{2,1,0:T(8,128)(2,1)}, bf16[5,8,8192]{2,1,0:T(8,128)(2,1)S(1)}, u32[]{:S(2)}, u32[]{:S(2)}) %collective-permute-start) | collective-permute-done | bytes 655392 | tf_op jit(solution)/shard_map/while/body/eval_jaxpr/ppermute | solution.py:25
  150.9 16.2 %collective-permute-done = bf16[5,8,8192]{2,1,0:T(8,128)(2,1)S(1)} collective-permute-done((bf16[5,8,8192]{2,1,0:T(8,128)(2,1)}, bf16[5,8,8192]{2,1,0:T(8,128)(2,1)S(1)}, u32[]{:S(2)}, u32[]{:S(2)}) %collective-permute-start) | collective-permute-done | bytes 655392 | tf_op jit(solution)/shard_map/while/body/eval_jaxpr/ppermute | solution.py:25
  170.7 47.8 %psum.7 = f32[8,8,5,4]{1,2,0,3:T(8,128)S(1)} all-reduce(f32[8,8,5,4]{1,2,0,3:T(8,128)S(1)} %copy.10), channel_id=1, replica_groups=mesh['bin'=8,'sky'=4] {'bin','sky'}, use_global_device_ids=true, to_apply=%region_10.11 | all-reduce | flops 1280 | bytes 10240 | tf_op jit(solution)/shard_map/psum | solution.py:157
  219.9 4.0 %fusion.78 = f32[5,8,8192]{2,1,0:T(8,128)S(1)} fusion(f32[5,8,8189]{2,1,0:T(8,128)} %get-tuple-element.843, f32[5,8,8189]{2,1,0:T(8,128)} %get-tuple-element.842, f32[5,8,8190]{2,1,0:T(8,128)} %get-tuple-element.841, f32[5,8,8190]{2,1,0:T(8,128)} %get-tuple-element.840, f32[5,8,8191]{2,1,0:T(8,128)} %get-tuple-element.839, ...), kind=kLoop, calls=%fused_computation.126 | loop fusion | flops 4915200 | bytes 9861328 | tf_op jit(solution)/shard_map/add | solution.py:76
  224.0 47.2 %while.43 = (s32[]{:T(128)}, f32[5,8,8192]{2,1,0:T(8,128)S(1)}, s32[]{:T(128)}, f32[8,8,5,4]{1,3,2,0:T(4,128)S(1)}, bf16[7,5,8,8192]{3,2,1,0:T(8,128)(2,1)}, /*i...) while((s32[]{:T(128)}, f32[5,8,8192]{2,1,0:T(8,128)S(1)}, ...), condition=%wide.region_12.13_spmd.clone.clone, body=%wide.region_11.12_spmd.clone.clone.sunk | while | flops 7554175 | bytes 28974256 | solution.py:179
  228.3 2.4 fusion.128
  235.0 2.4 fusion.128
  241.8 2.4 fusion.128
  248.5 2.4 fusion.128
  255.3 2.4 fusion.128
  262.0 2.4 fusion.128
  268.7 2.4 fusion.128
  271.2 5.9 %multiply_add_fusion.3 = f32[5,8,8192]{2,1,0:T(8,128)S(1)} fusion(f32[5,8,8192]{2,1,0:T(8,128)S(1)} %get-tuple-element.629, f32[5]{0:T(128)S(1)} %copy-done.9, f32[5]{0:T(128)S(1)} %copy-done.11, f32[5]{0:T(128)S(1)} %get-tuple-element.764, f32[5]{0:T(128)S(1)} %get-tuple-element.765, f32[5]{0:T(128)S(1)} %get-tuple-element.766, ...), kind=kLoop, calls=%fused_computation.127 | loop fusion | flops 10813440 | bytes 2621780 | tf_op jit(solution)/shard_map/add | solution.py:89
  277.1 5.3 %collective-permute-start.3 = (f32[5,8,8192]{2,1,0:T(8,128)S(1)}, f32[5,8,8192]{2,1,0:T(8,128)S(1)}, u32[]{:S(2)}, u32[]{:S(2)}) collective-permute-start(f32[5,8,8192]{2,1,0:T(8,128)S(1)} %multiply_add_fusion.3), channel_id=1, source_target_pairs={{0,1},{1,2},{2,3},{4,5},{5,6},{6,7},{8,9},{9,10},{10,11},{12,13},{... | collective-permute-start | bytes 3932168 | tf_op jit(solution)/shard_map/ppermute | solution.py:14
  282.4 1.9 collective-permute-start.4
  284.9 12.0 %collective-permute-done.3 = f32[5,8,8192]{2,1,0:T(8,128)S(1)} collective-permute-done((f32[5,8,8192]{2,1,0:T(8,128)S(1)}, f32[5,8,8192]{2,1,0:T(8,128)S(1)}, u32[]{:S(2)}, u32[]{:S(2)}) %collective-permute-start.3) | collective-permute-done | bytes 1310752 | tf_op jit(solution)/shard_map/ppermute | solution.py:14
  296.9 4.4 %collective-permute-done.4 = f32[5,8,8192]{2,1,0:T(8,128)S(1)} collective-permute-done((f32[5,8,8192]{2,1,0:T(8,128)S(1)}, f32[5,8,8192]{2,1,0:T(8,128)S(1)}, u32[]{:S(2)}, u32[]{:S(2)}) %collective-permute-start.4) | collective-permute-done | bytes 1310752 | tf_op jit(solution)/shard_map/ppermute | solution.py:17
  301.3 5.2 %fusion.36 = f32[8,8192]{1,0:T(8,128)} fusion(f32[5,8,8192]{2,1,0:T(8,128)S(1)} %multiply_add_fusion.3, f32[5,8,8192]{2,1,0:T(8,128)S(1)} %collective-permute-done.4, f32[5,8,8192]{2,1,0:T(8,128)S(1)} %collective-permute-done.3, f32[5]{0:T(128)S(1)} %copy-done.9, f32[5]{0:T(128)S(1)} %copy-done.11, f32[5]{0:T(128)S(1)} %get-tuple-element.764, ...), kind=kLoop, calls=%fused_computation.75 | loop fusion | flops 15663104 | bytes 4194644 | tf_op jit(solution)/shard_map/reduce_sum | solution.py:101
  (255 shorter events, 64.7 us)
Async XLA Ops:
  0.6 9.4 %collective-permute-start.1 = (bf16[8,8192]{1,0:T(8,128)(2,1)}, bf16[8,8192]{1,0:T(8,128)(2,1)S(1)}, u32[]{:S(2)}, u32[]{:S(2)}) collective-permute-start(bf16[8,8192]{1,0:T(8,128)(2,1)} %bitcast.118), channel_id=1, source_target_pairs={{0,1},{1,2},{2,3},{4,5},{5,6},{6,7},{8,9},{9,10},{10,11},{12,13},{... | collective-permute-start | bytes 393224 | tf_op jit(solution)/shard_map/ppermute | solution.py:14
  4.3 6.5 %collective-permute-start.2 = (bf16[8,8192]{1,0:T(8,128)(2,1)}, bf16[8,8192]{1,0:T(8,128)(2,1)S(1)}, u32[]{:S(2)}, u32[]{:S(2)}) collective-permute-start(bf16[8,8192]{1,0:T(8,128)(2,1)} %bitcast.119), channel_id=1, source_target_pairs={{1,0},{2,1},{3,2},{5,4},{6,5},{7,6},{9,8},{10,9},{11,10},{13,12},{... | collective-permute-start | bytes 393224 | tf_op jit(solution)/shard_map/ppermute | solution.py:17
  9.9 4.0 %copy-start.2 = (f32[5]{0:T(128)}, f32[5]{0:T(128)S(1)}, u32[]{:S(2)}) copy-start(f32[5]{0:T(128)S(1)} %get-tuple-element.775) | copy-start | bytes 64
  9.9 4.0 %copy-start.4 = (f32[5]{0:T(128)}, f32[5]{0:T(128)S(1)}, u32[]{:S(2)}) copy-start(f32[5]{0:T(128)S(1)} %get-tuple-element.776) | copy-start | bytes 64
  10.0 4.0 %copy-start.6 = (f32[5]{0:T(128)}, f32[5]{0:T(128)S(1)}, u32[]{:S(2)}) copy-start(f32[5]{0:T(128)S(1)} %get-tuple-element.777) | copy-start | bytes 64
  10.0 4.0 %copy-start.8 = (f32[5]{0:T(128)}, f32[5]{0:T(128)S(1)}, u32[]{:S(2)}) copy-start(f32[5]{0:T(128)S(1)} %get-tuple-element.778) | copy-start | bytes 64
  10.0 4.0 %copy-start.10 = (f32[5]{0:T(128)}, f32[5]{0:T(128)S(1)}, u32[]{:S(2)}) copy-start(f32[5]{0:T(128)S(1)} %get-tuple-element.779) | copy-start | bytes 64
  27.2 191.7 %copy-start = (f32[36,5,4]{0,2,1:T(4,128)S(1)}, f32[36,5,4]{0,2,1:T(4,128)}, u32[]{:S(2)}) copy-start(f32[36,5,4]{0,2,1:T(4,128)} %param.15) | copy-start | bytes 8644
  27.2 191.7 %copy-start.1 = (f32[36,5,4]{0,2,1:T(4,128)S(1)}, f32[36,5,4]{0,2,1:T(4,128)}, u32[]{:S(2)}) copy-start(f32[36,5,4]{0,2,1:T(4,128)} %param.14) | copy-start | bytes 8644
  27.2 15.4 %collective-permute-start = (bf16[5,8,8192]{2,1,0:T(8,128)(2,1)}, bf16[5,8,8192]{2,1,0:T(8,128)(2,1)S(1)}, u32[]{:S(2)}, u32[]{:S(2)}) collective-permute-start(bf16[5,8,8192]{2,1,0:T(8,128)(2,1)} %get-tuple-element.1039), channel_id=1, source_target_pairs={{0,4},{4,8},{8,12},{12,16},{16,20},{20,24},{24,28},{28,0},{1,5},{5... | collective-permute-start | bytes 1966088 | tf_op jit(solution)/shard_map/while/body/eval_jaxpr/ppermute | solution.py:25
  46.2 16.5 %collective-permute-start = (bf16[5,8,8192]{2,1,0:T(8,128)(2,1)}, bf16[5,8,8192]{2,1,0:T(8,128)(2,1)S(1)}, u32[]{:S(2)}, u32[]{:S(2)}) collective-permute-start(bf16[5,8,8192]{2,1,0:T(8,128)(2,1)} %get-tuple-element.1039), channel_id=1, source_target_pairs={{0,4},{4,8},{8,12},{12,16},{16,20},{20,24},{24,28},{28,0},{1,5},{5... | collective-permute-start | bytes 1966088 | tf_op jit(solution)/shard_map/while/body/eval_jaxpr/ppermute | solution.py:25
  66.3 17.8 %collective-permute-start = (bf16[5,8,8192]{2,1,0:T(8,128)(2,1)}, bf16[5,8,8192]{2,1,0:T(8,128)(2,1)S(1)}, u32[]{:S(2)}, u32[]{:S(2)}) collective-permute-start(bf16[5,8,8192]{2,1,0:T(8,128)(2,1)} %get-tuple-element.1039), channel_id=1, source_target_pairs={{0,4},{4,8},{8,12},{12,16},{16,20},{20,24},{24,28},{28,0},{1,5},{5... | collective-permute-start | bytes 1966088 | tf_op jit(solution)/shard_map/while/body/eval_jaxpr/ppermute | solution.py:25
  87.7 17.0 %collective-permute-start = (bf16[5,8,8192]{2,1,0:T(8,128)(2,1)}, bf16[5,8,8192]{2,1,0:T(8,128)(2,1)S(1)}, u32[]{:S(2)}, u32[]{:S(2)}) collective-permute-start(bf16[5,8,8192]{2,1,0:T(8,128)(2,1)} %get-tuple-element.1039), channel_id=1, source_target_pairs={{0,4},{4,8},{8,12},{12,16},{16,20},{20,24},{24,28},{28,0},{1,5},{5... | collective-permute-start | bytes 1966088 | tf_op jit(solution)/shard_map/while/body/eval_jaxpr/ppermute | solution.py:25
  108.3 18.2 %collective-permute-start = (bf16[5,8,8192]{2,1,0:T(8,128)(2,1)}, bf16[5,8,8192]{2,1,0:T(8,128)(2,1)S(1)}, u32[]{:S(2)}, u32[]{:S(2)}) collective-permute-start(bf16[5,8,8192]{2,1,0:T(8,128)(2,1)} %get-tuple-element.1039), channel_id=1, source_target_pairs={{0,4},{4,8},{8,12},{12,16},{16,20},{20,24},{24,28},{28,0},{1,5},{5... | collective-permute-start | bytes 1966088 | tf_op jit(solution)/shard_map/while/body/eval_jaxpr/ppermute | solution.py:25
  130.1 17.1 %collective-permute-start = (bf16[5,8,8192]{2,1,0:T(8,128)(2,1)}, bf16[5,8,8192]{2,1,0:T(8,128)(2,1)S(1)}, u32[]{:S(2)}, u32[]{:S(2)}) collective-permute-start(bf16[5,8,8192]{2,1,0:T(8,128)(2,1)} %get-tuple-element.1039), channel_id=1, source_target_pairs={{0,4},{4,8},{8,12},{12,16},{16,20},{20,24},{24,28},{28,0},{1,5},{5... | collective-permute-start | bytes 1966088 | tf_op jit(solution)/shard_map/while/body/eval_jaxpr/ppermute | solution.py:25
  150.8 16.2 %collective-permute-start = (bf16[5,8,8192]{2,1,0:T(8,128)(2,1)}, bf16[5,8,8192]{2,1,0:T(8,128)(2,1)S(1)}, u32[]{:S(2)}, u32[]{:S(2)}) collective-permute-start(bf16[5,8,8192]{2,1,0:T(8,128)(2,1)} %get-tuple-element.1039), channel_id=1, source_target_pairs={{0,4},{4,8},{8,12},{12,16},{16,20},{20,24},{24,28},{28,0},{1,5},{5... | collective-permute-start | bytes 1966088 | tf_op jit(solution)/shard_map/while/body/eval_jaxpr/ppermute | solution.py:25
  223.9 47.2 %copy-start.3 = (f32[5]{0:T(128)S(1)}, f32[5]{0:T(128)}, u32[]{:S(2)}) copy-start(f32[5]{0:T(128)} %copy-done.2) | copy-start | bytes 64
  223.9 47.2 %copy-start.5 = (f32[5]{0:T(128)S(1)}, f32[5]{0:T(128)}, u32[]{:S(2)}) copy-start(f32[5]{0:T(128)} %copy-done.4) | copy-start | bytes 64
  223.9 47.2 %copy-start.7 = (f32[5]{0:T(128)S(1)}, f32[5]{0:T(128)}, u32[]{:S(2)}) copy-start(f32[5]{0:T(128)} %copy-done.6) | copy-start | bytes 64
  223.9 47.2 %copy-start.9 = (f32[5]{0:T(128)S(1)}, f32[5]{0:T(128)}, u32[]{:S(2)}) copy-start(f32[5]{0:T(128)} %copy-done.8) | copy-start | bytes 64
  224.0 47.2 %copy-start.11 = (f32[5]{0:T(128)S(1)}, f32[5]{0:T(128)}, u32[]{:S(2)}) copy-start(f32[5]{0:T(128)} %copy-done.10) | copy-start | bytes 64
  277.1 19.8 %collective-permute-start.3 = (f32[5,8,8192]{2,1,0:T(8,128)S(1)}, f32[5,8,8192]{2,1,0:T(8,128)S(1)}, u32[]{:S(2)}, u32[]{:S(2)}) collective-permute-start(f32[5,8,8192]{2,1,0:T(8,128)S(1)} %multiply_add_fusion.3), channel_id=1, source_target_pairs={{0,1},{1,2},{2,3},{4,5},{5,6},{6,7},{8,9},{9,10},{10,11},{12,13},{... | collective-permute-start | bytes 3932168 | tf_op jit(solution)/shard_map/ppermute | solution.py:14
  282.4 18.9 %collective-permute-start.4 = (f32[5,8,8192]{2,1,0:T(8,128)S(1)}, f32[5,8,8192]{2,1,0:T(8,128)S(1)}, u32[]{:S(2)}, u32[]{:S(2)}) collective-permute-start(f32[5,8,8192]{2,1,0:T(8,128)S(1)} %multiply_add_fusion.3), channel_id=1, source_target_pairs={{1,0},{2,1},{3,2},{5,4},{6,5},{7,6},{9,8},{10,9},{11,10},{13,12},{... | collective-permute-start | bytes 3932168 | tf_op jit(solution)/shard_map/ppermute | solution.py:17
where the time goes:
time: 307 us; the launch traced here: 306 us
  waiting for transfers between devices  133 us (43%)
  other arithmetic  79.3 us (26%)
  blocking collectives  47.8 us (16%)
  local copies, waits for them, and re-layouts  22 us (7%)
  starting transfers between devices  14.4 us (5%)
  matrix products  8.21 us (3%)
    ppermute x7, waiting for transfers between devices, shifted(): return lax.ppermute(value, axis, pairs)  116 us
    psum x1, blocking collectives, per_device(): pair_table = lax.psum(tables, ('bin', 'sky'))  47.8 us
    add x7, other arithmetic, reread(): return totals + partner_term(visitor, k)  16.7 us
    mul x24, other arithmetic, adjoint_lags(): joint_mask[None] * widened[:, :, offset:]  14.7 us
    ppermute x2, waiting for transfers between devices, with_halo(): lax.ppermute(lax.slice_in_dim(block, block.shape[dim] - width, None, axis...  12 us
    reduce_sum x29, other arithmetic, lagged(): columns.append(jnp.sum(product, axis=(1, 2)))  11.9 us
    while x42, local copies, waits for them, and re-layouts  8.95 us
    ppermute x2, starting transfers between devices, with_halo(): lax.ppermute(lax.slice_in_dim(block, block.shape[dim] - width, None, axis...  8.95 us
  transfers between devices with their start and end apart: 11, of which 10 were waited for; matrix products, arithmetic and copies ran while one was open for 2% of the time, Pallas kernels for 0%

commit v1 on v0

--- a/solution.py
+++ b/solution.py
@@ -154,7 +154,7 @@
         return (carried, tables, stored)
 
     _, tables, stored = lax.fori_loop(1, bin_count, advance, (own_maps, initial, stored_init))
-    pair_table = lax.psum(tables, ("bin", "sky"))
+    pair_table = jax.lax.psum(jax.lax.psum(tables, "sky"), "bin")
     left_hot = (bin_pairs[:, 0:1] == indices[None, :]).astype(jnp.float32)
     right_hot = (bin_pairs[:, 1:2] == indices[None, :]).astype(jnp.float32)
     corr_table = jnp.einsum("pi,pj,ijsl->psl", left_hot, right_hot, pair_table, precision=HIGH)

time: 307 us -> 312 us (1.016); the launches traced: 306 us -> 308 us
  starting transfers between devices: 14.4 us -> 18.6 us
    ppermute x2, starting transfers between devices: 8.95 us -> 13.1 us  [with_halo(): lax.ppermute(lax.slice_in_dim(block, block.shape[dim] - width, None, axis...]
    psum x1 -> x2, blocking collectives: 47.8 us -> 45 us  [per_device(): pair_table = jax.lax.psum(jax.lax.psum(tables, 'sky'), 'bin')]
where the time goes in v1:
time: 312 us; the launch traced here: 308 us
  waiting for transfers between devices  133 us (43%)
  other arithmetic  79.3 us (25%)
  blocking collectives  45 us (14%)
  local copies, waits for them, and re-layouts  22 us (7%)
  starting transfers between devices  18.6 us (6%)
  matrix products  8.21 us (3%)
    ppermute x7, waiting for transfers between devices, shifted(): return lax.ppermute(value, axis, pairs)  116 us
    psum x2, blocking collectives, per_device(): pair_table = jax.lax.psum(jax.lax.psum(tables, 'sky'), 'bin')  45 us
    add x7, other arithmetic, reread(): return totals + partner_term(visitor, k)  16.7 us
    mul x24, other arithmetic, adjoint_lags(): joint_mask[None] * widened[:, :, offset:]  14.7 us
    ppermute x2, starting transfers between devices, with_halo(): lax.ppermute(lax.slice_in_dim(block, block.shape[dim] - width, None, axis...  13.1 us
    ppermute x2, waiting for transfers between devices, with_halo(): lax.ppermute(lax.slice_in_dim(block, block.shape[dim] - width, None, axis...  12 us
    reduce_sum x29, other arithmetic, lagged(): columns.append(jnp.sum(product, axis=(1, 2)))  11.9 us
    while x42, local copies, waits for them, and re-layouts  8.95 us
  transfers between devices with their start and end apart: 11, of which 10 were waited for; matrix products, arithmetic and copies ran while one was open for 2% of the time, Pallas kernels for 0%

profile of v1, /device:TPU:9, one launch (start us, length us, event | category | flops | bytes accessed | tf_op | source)
XLA Modules:
  0.0 307.9 jit_solution(15167162142738725953)
XLA Ops:
  0.6 3.7 %collective-permute-start.1 = (bf16[8,8192]{1,0:T(8,128)(2,1)}, bf16[8,8192]{1,0:T(8,128)(2,1)S(1)}, u32[]{:S(2)}, u32[]{:S(2)}) collective-permute-start(bf16[8,8192]{1,0:T(8,128)(2,1)} %bitcast.118), channel_id=1, source_target_pairs={{0,1},{1,2},{2,3},{4,5},{5,6},{6,7},{8,9},{9,10},{10,11},{12,13},{... | collective-permute-start | bytes 393224 | tf_op jit(solution)/shard_map/ppermute | solution.py:14
  4.3 1.9 collective-permute-start.2
  8.1 1.8 slice_reduce_fusion.16
  12.1 1.8 multiply_add_fusion.4
  14.0 5.9 %fusion.112 = (f32[5,8,8192]{2,1,0:T(8,128)S(1)}, bf16[5,8,8192]{2,1,0:T(8,128)(2,1)S(1)}) fusion(f32[5]{0:T(128)S(1)} %get-tuple-element.778, f32[5]{0:T(128)S(1)} %get-tuple-element.779, f32[5]{0:T(128)S(1)} %get-tuple-element.764, f32[5]{0:T(128)S(1)} %get-tuple-element.765, f32[5]{0:T(128)S(1)} %get-tuple-element.766, f32[5]{0:T(128)S(1)} %get-tuple-element.767, ...), kind=kLoop, calls=%fused_computation.223 | loop fusion | flops 11468800 | bytes 3277140 | tf_op jit(solution)/shard_map/convert_element_type | solution.py:57
  22.5 2.1 slice_multiply_fusion.9
  24.6 2.1 slice_multiply_fusion.7
  27.2 143.4 %while.42 = (s32[]{:T(128)}, bf16[5,8,8192]{2,1,0:T(8,128)(2,1)}, f32[8,8,5,4]{1,3,2,0:T(4,128)S(1)}, bf16[7,5,8,8192]{3,2,1,0:T(8,128)(2,1)}, s32[]{:T(128)}, /...) while((s32[]{:T(128)}, bf16[5,8,8192]{2,1,0:T(8,128)(2,1)}, ...), condition=%wide.region_9.10_spmd.clone.clone, body=%wide.region_4.9_spmd.clone.clone.sunk | while | flops 6555130 | bytes 10627522 | solution.py:156
  28.6 14.0 %collective-permute-done = bf16[5,8,8192]{2,1,0:T(8,128)(2,1)S(1)} collective-permute-done((bf16[5,8,8192]{2,1,0:T(8,128)(2,1)}, bf16[5,8,8192]{2,1,0:T(8,128)(2,1)S(1)}, u32[]{:S(2)}, u32[]{:S(2)}) %collective-permute-start) | collective-permute-done | bytes 655392 | tf_op jit(solution)/shard_map/while/body/eval_jaxpr/ppermute | solution.py:25
  46.6 16.1 %collective-permute-done = bf16[5,8,8192]{2,1,0:T(8,128)(2,1)S(1)} collective-permute-done((bf16[5,8,8192]{2,1,0:T(8,128)(2,1)}, bf16[5,8,8192]{2,1,0:T(8,128)(2,1)S(1)}, u32[]{:S(2)}, u32[]{:S(2)}) %collective-permute-start) | collective-permute-done | bytes 655392 | tf_op jit(solution)/shard_map/while/body/eval_jaxpr/ppermute | solution.py:25
  66.4 17.7 %collective-permute-done = bf16[5,8,8192]{2,1,0:T(8,128)(2,1)S(1)} collective-permute-done((bf16[5,8,8192]{2,1,0:T(8,128)(2,1)}, bf16[5,8,8192]{2,1,0:T(8,128)(2,1)S(1)}, u32[]{:S(2)}, u32[]{:S(2)}) %collective-permute-start) | collective-permute-done | bytes 655392 | tf_op jit(solution)/shard_map/while/body/eval_jaxpr/ppermute | solution.py:25
  87.8 16.9 %collective-permute-done = bf16[5,8,8192]{2,1,0:T(8,128)(2,1)S(1)} collective-permute-done((bf16[5,8,8192]{2,1,0:T(8,128)(2,1)}, bf16[5,8,8192]{2,1,0:T(8,128)(2,1)S(1)}, u32[]{:S(2)}, u32[]{:S(2)}) %collective-permute-start) | collective-permute-done | bytes 655392 | tf_op jit(solution)/shard_map/while/body/eval_jaxpr/ppermute | solution.py:25
  108.4 18.1 %collective-permute-done = bf16[5,8,8192]{2,1,0:T(8,128)(2,1)S(1)} collective-permute-done((bf16[5,8,8192]{2,1,0:T(8,128)(2,1)}, bf16[5,8,8192]{2,1,0:T(8,128)(2,1)S(1)}, u32[]{:S(2)}, u32[]{:S(2)}) %collective-permute-start) | collective-permute-done | bytes 655392 | tf_op jit(solution)/shard_map/while/body/eval_jaxpr/ppermute | solution.py:25
  130.2 17.0 %collective-permute-done = bf16[5,8,8192]{2,1,0:T(8,128)(2,1)S(1)} collective-permute-done((bf16[5,8,8192]{2,1,0:T(8,128)(2,1)}, bf16[5,8,8192]{2,1,0:T(8,128)(2,1)S(1)}, u32[]{:S(2)}, u32[]{:S(2)}) %collective-permute-start) | collective-permute-done | bytes 655392 | tf_op jit(solution)/shard_map/while/body/eval_jaxpr/ppermute | solution.py:25
  150.9 16.2 %collective-permute-done = bf16[5,8,8192]{2,1,0:T(8,128)(2,1)S(1)} collective-permute-done((bf16[5,8,8192]{2,1,0:T(8,128)(2,1)}, bf16[5,8,8192]{2,1,0:T(8,128)(2,1)S(1)}, u32[]{:S(2)}, u32[]{:S(2)}) %collective-permute-start) | collective-permute-done | bytes 655392 | tf_op jit(solution)/shard_map/while/body/eval_jaxpr/ppermute | solution.py:25
  170.7 13.8 %psum.14 = f32[8,8,5,4]{1,2,0,3:T(8,128)S(1)} all-reduce(f32[8,8,5,4]{1,2,0,3:T(8,128)S(1)} %copy.10), channel_id=1, replica_groups=mesh['bin'=8,'sky'=4] {'sky'}, use_global_device_ids=true, to_apply=%region_10.11 | all-reduce | flops 1280 | bytes 10240 | tf_op jit(solution)/shard_map/psum | solution.py:157
  184.4 31.2 %psum.15 = f32[8,8,5,4]{1,2,0,3:T(8,128)S(1)} all-reduce(f32[8,8,5,4]{1,2,0,3:T(8,128)S(1)} %psum.14), channel_id=1, replica_groups=mesh['bin'=8,'sky'=4] {'bin'}, use_global_device_ids=true, to_apply=%region_11.12 | all-reduce | flops 1280 | bytes 10240 | tf_op jit(solution)/shard_map/psum | solution.py:157
  217.1 4.0 %fusion.78 = f32[5,8,8192]{2,1,0:T(8,128)S(1)} fusion(f32[5,8,8189]{2,1,0:T(8,128)} %get-tuple-element.843, f32[5,8,8189]{2,1,0:T(8,128)} %get-tuple-element.842, f32[5,8,8190]{2,1,0:T(8,128)} %get-tuple-element.841, f32[5,8,8190]{2,1,0:T(8,128)} %get-tuple-element.840, f32[5,8,8191]{2,1,0:T(8,128)} %get-tuple-element.839, ...), kind=kLoop, calls=%fused_computation.126 | loop fusion | flops 4915200 | bytes 9861328 | tf_op jit(solution)/shard_map/add | solution.py:76
  221.2 47.2 %while.43 = (s32[]{:T(128)}, f32[5,8,8192]{2,1,0:T(8,128)S(1)}, s32[]{:T(128)}, f32[8,8,5,4]{1,3,2,0:T(4,128)S(1)}, bf16[7,5,8,8192]{3,2,1,0:T(8,128)(2,1)}, /*i...) while((s32[]{:T(128)}, f32[5,8,8192]{2,1,0:T(8,128)S(1)}, ...), condition=%wide.region_13.14_spmd.clone.clone, body=%wide.region_12.13_spmd.clone.clone.sunk | while | flops 7554175 | bytes 28974256 | solution.py:179
  225.5 2.4 fusion.128
  232.3 2.4 fusion.128
  239.0 2.4 fusion.128
  245.7 2.4 fusion.128
  252.5 2.4 fusion.128
  259.2 2.4 fusion.128
  266.0 2.4 fusion.128
  268.4 5.9 %multiply_add_fusion.3 = f32[5,8,8192]{2,1,0:T(8,128)S(1)} fusion(f32[5,8,8192]{2,1,0:T(8,128)S(1)} %get-tuple-element.629, f32[5]{0:T(128)S(1)} %copy-done.9, f32[5]{0:T(128)S(1)} %copy-done.11, f32[5]{0:T(128)S(1)} %get-tuple-element.764, f32[5]{0:T(128)S(1)} %get-tuple-element.765, f32[5]{0:T(128)S(1)} %get-tuple-element.766, ...), kind=kLoop, calls=%fused_computation.127 | loop fusion | flops 10813440 | bytes 2621780 | tf_op jit(solution)/shard_map/add | solution.py:89
  274.4 9.5 %collective-permute-start.3 = (f32[5,8,8192]{2,1,0:T(8,128)S(1)}, f32[5,8,8192]{2,1,0:T(8,128)S(1)}, u32[]{:S(2)}, u32[]{:S(2)}) collective-permute-start(f32[5,8,8192]{2,1,0:T(8,128)S(1)} %multiply_add_fusion.3), channel_id=1, source_target_pairs={{0,1},{1,2},{2,3},{4,5},{5,6},{6,7},{8,9},{9,10},{10,11},{12,13},{... | collective-permute-start | bytes 3932168 | tf_op jit(solution)/shard_map/ppermute | solution.py:14
  283.8 1.9 collective-permute-start.4
  286.4 12.0 %collective-permute-done.3 = f32[5,8,8192]{2,1,0:T(8,128)S(1)} collective-permute-done((f32[5,8,8192]{2,1,0:T(8,128)S(1)}, f32[5,8,8192]{2,1,0:T(8,128)S(1)}, u32[]{:S(2)}, u32[]{:S(2)}) %collective-permute-start.3) | collective-permute-done | bytes 1310752 | tf_op jit(solution)/shard_map/ppermute | solution.py:14
  298.4 4.4 %collective-permute-done.4 = f32[5,8,8192]{2,1,0:T(8,128)S(1)} collective-permute-done((f32[5,8,8192]{2,1,0:T(8,128)S(1)}, f32[5,8,8192]{2,1,0:T(8,128)S(1)}, u32[]{:S(2)}, u32[]{:S(2)}) %collective-permute-start.4) | collective-permute-done | bytes 1310752 | tf_op jit(solution)/shard_map/ppermute | solution.py:17
  302.7 5.2 %fusion.36 = f32[8,8192]{1,0:T(8,128)} fusion(f32[5,8,8192]{2,1,0:T(8,128)S(1)} %multiply_add_fusion.3, f32[5,8,8192]{2,1,0:T(8,128)S(1)} %collective-permute-done.4, f32[5,8,8192]{2,1,0:T(8,128)S(1)} %collective-permute-done.3, f32[5]{0:T(128)S(1)} %copy-done.9, f32[5]{0:T(128)S(1)} %copy-done.11, f32[5]{0:T(128)S(1)} %get-tuple-element.764, ...), kind=kLoop, calls=%fused_computation.75 | loop fusion | flops 15663104 | bytes 4194644 | tf_op jit(solution)/shard_map/reduce_sum | solution.py:101
  (256 shorter events, 66.4 us)
Async XLA Ops:
  0.6 9.4 %collective-permute-start.1 = (bf16[8,8192]{1,0:T(8,128)(2,1)}, bf16[8,8192]{1,0:T(8,128)(2,1)S(1)}, u32[]{:S(2)}, u32[]{:S(2)}) collective-permute-start(bf16[8,8192]{1,0:T(8,128)(2,1)} %bitcast.118), channel_id=1, source_target_pairs={{0,1},{1,2},{2,3},{4,5},{5,6},{6,7},{8,9},{9,10},{10,11},{12,13},{... | collective-permute-start | bytes 393224 | tf_op jit(solution)/shard_map/ppermute | solution.py:14
  4.3 6.5 %collective-permute-start.2 = (bf16[8,8192]{1,0:T(8,128)(2,1)}, bf16[8,8192]{1,0:T(8,128)(2,1)S(1)}, u32[]{:S(2)}, u32[]{:S(2)}) collective-permute-start(bf16[8,8192]{1,0:T(8,128)(2,1)} %bitcast.119), channel_id=1, source_target_pairs={{1,0},{2,1},{3,2},{5,4},{6,5},{7,6},{9,8},{10,9},{11,10},{13,12},{... | collective-permute-start | bytes 393224 | tf_op jit(solution)/shard_map/ppermute | solution.py:17
  9.9 4.0 %copy-start.2 = (f32[5]{0:T(128)}, f32[5]{0:T(128)S(1)}, u32[]{:S(2)}) copy-start(f32[5]{0:T(128)S(1)} %get-tuple-element.775) | copy-start | bytes 64
  9.9 4.0 %copy-start.4 = (f32[5]{0:T(128)}, f32[5]{0:T(128)S(1)}, u32[]{:S(2)}) copy-start(f32[5]{0:T(128)S(1)} %get-tuple-element.776) | copy-start | bytes 64
  10.0 4.0 %copy-start.6 = (f32[5]{0:T(128)}, f32[5]{0:T(128)S(1)}, u32[]{:S(2)}) copy-start(f32[5]{0:T(128)S(1)} %get-tuple-element.777) | copy-start | bytes 64
  10.0 4.0 %copy-start.8 = (f32[5]{0:T(128)}, f32[5]{0:T(128)S(1)}, u32[]{:S(2)}) copy-start(f32[5]{0:T(128)S(1)} %get-tuple-element.778) | copy-start | bytes 64
  10.0 4.0 %copy-start.10 = (f32[5]{0:T(128)}, f32[5]{0:T(128)S(1)}, u32[]{:S(2)}) copy-start(f32[5]{0:T(128)S(1)} %get-tuple-element.779) | copy-start | bytes 64
  27.2 188.9 %copy-start = (f32[36,5,4]{0,2,1:T(4,128)S(1)}, f32[36,5,4]{0,2,1:T(4,128)}, u32[]{:S(2)}) copy-start(f32[36,5,4]{0,2,1:T(4,128)} %param.15) | copy-start | bytes 8644
  27.2 188.9 %copy-start.1 = (f32[36,5,4]{0,2,1:T(4,128)S(1)}, f32[36,5,4]{0,2,1:T(4,128)}, u32[]{:S(2)}) copy-start(f32[36,5,4]{0,2,1:T(4,128)} %param.14) | copy-start | bytes 8644
  27.2 15.4 %collective-permute-start = (bf16[5,8,8192]{2,1,0:T(8,128)(2,1)}, bf16[5,8,8192]{2,1,0:T(8,128)(2,1)S(1)}, u32[]{:S(2)}, u32[]{:S(2)}) collective-permute-start(bf16[5,8,8192]{2,1,0:T(8,128)(2,1)} %get-tuple-element.1039), channel_id=1, source_target_pairs={{0,4},{4,8},{8,12},{12,16},{16,20},{20,24},{24,28},{28,0},{1,5},{5... | collective-permute-start | bytes 1966088 | tf_op jit(solution)/shard_map/while/body/eval_jaxpr/ppermute | solution.py:25
  46.2 16.5 %collective-permute-start = (bf16[5,8,8192]{2,1,0:T(8,128)(2,1)}, bf16[5,8,8192]{2,1,0:T(8,128)(2,1)S(1)}, u32[]{:S(2)}, u32[]{:S(2)}) collective-permute-start(bf16[5,8,8192]{2,1,0:T(8,128)(2,1)} %get-tuple-element.1039), channel_id=1, source_target_pairs={{0,4},{4,8},{8,12},{12,16},{16,20},{20,24},{24,28},{28,0},{1,5},{5... | collective-permute-start | bytes 1966088 | tf_op jit(solution)/shard_map/while/body/eval_jaxpr/ppermute | solution.py:25
  66.3 17.8 %collective-permute-start = (bf16[5,8,8192]{2,1,0:T(8,128)(2,1)}, bf16[5,8,8192]{2,1,0:T(8,128)(2,1)S(1)}, u32[]{:S(2)}, u32[]{:S(2)}) collective-permute-start(bf16[5,8,8192]{2,1,0:T(8,128)(2,1)} %get-tuple-element.1039), channel_id=1, source_target_pairs={{0,4},{4,8},{8,12},{12,16},{16,20},{20,24},{24,28},{28,0},{1,5},{5... | collective-permute-start | bytes 1966088 | tf_op jit(solution)/shard_map/while/body/eval_jaxpr/ppermute | solution.py:25
  87.7 17.0 %collective-permute-start = (bf16[5,8,8192]{2,1,0:T(8,128)(2,1)}, bf16[5,8,8192]{2,1,0:T(8,128)(2,1)S(1)}, u32[]{:S(2)}, u32[]{:S(2)}) collective-permute-start(bf16[5,8,8192]{2,1,0:T(8,128)(2,1)} %get-tuple-element.1039), channel_id=1, source_target_pairs={{0,4},{4,8},{8,12},{12,16},{16,20},{20,24},{24,28},{28,0},{1,5},{5... | collective-permute-start | bytes 1966088 | tf_op jit(solution)/shard_map/while/body/eval_jaxpr/ppermute | solution.py:25
  108.3 18.2 %collective-permute-start = (bf16[5,8,8192]{2,1,0:T(8,128)(2,1)}, bf16[5,8,8192]{2,1,0:T(8,128)(2,1)S(1)}, u32[]{:S(2)}, u32[]{:S(2)}) collective-permute-start(bf16[5,8,8192]{2,1,0:T(8,128)(2,1)} %get-tuple-element.1039), channel_id=1, source_target_pairs={{0,4},{4,8},{8,12},{12,16},{16,20},{20,24},{24,28},{28,0},{1,5},{5... | collective-permute-start | bytes 1966088 | tf_op jit(solution)/shard_map/while/body/eval_jaxpr/ppermute | solution.py:25
  130.1 17.1 %collective-permute-start = (bf16[5,8,8192]{2,1,0:T(8,128)(2,1)}, bf16[5,8,8192]{2,1,0:T(8,128)(2,1)S(1)}, u32[]{:S(2)}, u32[]{:S(2)}) collective-permute-start(bf16[5,8,8192]{2,1,0:T(8,128)(2,1)} %get-tuple-element.1039), channel_id=1, source_target_pairs={{0,4},{4,8},{8,12},{12,16},{16,20},{20,24},{24,28},{28,0},{1,5},{5... | collective-permute-start | bytes 1966088 | tf_op jit(solution)/shard_map/while/body/eval_jaxpr/ppermute | solution.py:25
  150.8 16.2 %collective-permute-start = (bf16[5,8,8192]{2,1,0:T(8,128)(2,1)}, bf16[5,8,8192]{2,1,0:T(8,128)(2,1)S(1)}, u32[]{:S(2)}, u32[]{:S(2)}) collective-permute-start(bf16[5,8,8192]{2,1,0:T(8,128)(2,1)} %get-tuple-element.1039), channel_id=1, source_target_pairs={{0,4},{4,8},{8,12},{12,16},{16,20},{20,24},{24,28},{28,0},{1,5},{5... | collective-permute-start | bytes 1966088 | tf_op jit(solution)/shard_map/while/body/eval_jaxpr/ppermute | solution.py:25
  221.1 47.2 %copy-start.3 = (f32[5]{0:T(128)S(1)}, f32[5]{0:T(128)}, u32[]{:S(2)}) copy-start(f32[5]{0:T(128)} %copy-done.2) | copy-start | bytes 64
  221.1 47.2 %copy-start.5 = (f32[5]{0:T(128)S(1)}, f32[5]{0:T(128)}, u32[]{:S(2)}) copy-start(f32[5]{0:T(128)} %copy-done.4) | copy-start | bytes 64
  221.2 47.2 %copy-start.7 = (f32[5]{0:T(128)S(1)}, f32[5]{0:T(128)}, u32[]{:S(2)}) copy-start(f32[5]{0:T(128)} %copy-done.6) | copy-start | bytes 64
  221.2 47.2 %copy-start.9 = (f32[5]{0:T(128)S(1)}, f32[5]{0:T(128)}, u32[]{:S(2)}) copy-start(f32[5]{0:T(128)} %copy-done.8) | copy-start | bytes 64
  221.2 47.2 %copy-start.11 = (f32[5]{0:T(128)S(1)}, f32[5]{0:T(128)}, u32[]{:S(2)}) copy-start(f32[5]{0:T(128)} %copy-done.10) | copy-start | bytes 64
  274.4 24.0 %collective-permute-start.3 = (f32[5,8,8192]{2,1,0:T(8,128)S(1)}, f32[5,8,8192]{2,1,0:T(8,128)S(1)}, u32[]{:S(2)}, u32[]{:S(2)}) collective-permute-start(f32[5,8,8192]{2,1,0:T(8,128)S(1)} %multiply_add_fusion.3), channel_id=1, source_target_pairs={{0,1},{1,2},{2,3},{4,5},{5,6},{6,7},{8,9},{9,10},{10,11},{12,13},{... | collective-permute-start | bytes 3932168 | tf_op jit(solution)/shard_map/ppermute | solution.py:14
  283.8 18.9 %collective-permute-start.4 = (f32[5,8,8192]{2,1,0:T(8,128)S(1)}, f32[5,8,8192]{2,1,0:T(8,128)S(1)}, u32[]{:S(2)}, u32[]{:S(2)}) collective-permute-start(f32[5,8,8192]{2,1,0:T(8,128)S(1)} %multiply_add_fusion.3), channel_id=1, source_target_pairs={{1,0},{2,1},{3,2},{5,4},{6,5},{7,6},{9,8},{10,9},{11,10},{13,12},{... | collective-permute-start | bytes 3932168 | tf_op jit(solution)/shard_map/ppermute | solution.py:17
